TPU v7x, 32 devices: a whole 2x2x4 slice. The times are simulated.
32 devices in a mesh: dir: 2 (over y), dp: 16 (over z, x, core).
Axes of the slice: x: 2, y: 2, z: 4, core: 2. Of those that a mesh axis runs over, the one named last changes fastest.
Arguments:
- tokens: bfloat16 [16, 1024, 768], P('dp', 'dir'), may hold values from -6 to 6
- norm_gain: float32 [768], replicated, may hold values from 0.5 to 1.5
- w_zx: bfloat16 [768, 3072], P('dp'), may hold values from -0.21875 to 0.21875
- w_bc: bfloat16 [768, 128], P('dp'), may hold values from -0.21875 to 0.21875
- w_dt: bfloat16 [768, 48], P('dp'), may hold values from -0.21875 to 0.21875
- conv_w: float32 [4, 1664], replicated, may hold values from -3 to 3
- conv_b: float32 [1664], replicated, may hold values from -1.75 to 1.75
- dt_bias: float32 [48], replicated, may hold values from -4.5 to -2
- a_log: float32 [48], replicated, may hold values from -2.5 to 1.5
- d_skip: float32 [24], replicated, may hold values from 0.5 to 1.5
- out_gain: float32 [1536], replicated, may hold values from 0.5 to 1.5
- w_out: bfloat16 [1536, 768], P('dp'), may hold values from -0.15625 to 0.15625
- doc_lengths: int32 [16, 4], P('dp'), may hold values from 1 to 512, 1024 in all within a row
- out_grad: bfloat16 [16, 1024, 768], P('dp', 'dir'), may hold values from -6 to 6
Outputs:
- block_out: bfloat16 [16, 1024, 768], P('dp', 'dir')
- grad_tokens: bfloat16 [16, 1024, 768], P('dp', 'dir')
- grad_norm_gain: float32 [768], replicated
- grad_w_zx: float32 [768, 3072], replicated
- grad_w_bc: float32 [768, 128], replicated
- grad_w_dt: float32 [768, 48], replicated
- grad_conv_w: float32 [4, 1664], replicated
- grad_conv_b: float32 [1664], replicated
- grad_dt_bias: float32 [48], replicated
- grad_a_log: float32 [48], replicated
- grad_d_skip: float32 [24], replicated
- grad_out_gain: float32 [1536], replicated
- grad_w_out: float32 [1536, 768], replicated
Inputs may be any that keep to these rules, and one draw needn't show every extreme that they name: `doc_lengths`: in each row the 4 lengths sum to 1024, and the longest is exactly 512.
All inputs are finite; a program needn't handle non-finite values.
Results may differ from a plain program's by a relative error of at most 0.014.
Values may be sent and summed in bfloat16 or wider, within the bound.
No kernel may reach another device: no remote copies, remote signals or barrier semaphores. Data moves between devices by JAX's collectives and lax.ppermute only.
A program may use at most 192 MiB of HBM per device.

v0:
```python
from functools import partial
import jax
import jax.numpy as jnp
from jax import lax
from jax.sharding import PartitionSpec as P

D = 768
HEADS = 24
HEADDIM = 64
STATE = 64
INNER = 1536
BLOCK = 128
CONV = 4
LEN = 1024
highest = lax.Precision.HIGHEST
epsilon = 1e-05


def shifted_2(block, axis, distance):
    devices = range(lax.axis_size(axis))
    route = [(i - distance, i) for i in devices if i - distance in devices]
    return lax.ppermute(block, axis, route)


def partner(shard, axis, stride):
    return lax.ppermute(shard, axis, [(i, i ^ 1 << stride) for i in range(lax.axis_size(axis))])


def segment_ids(lengths_row, length):
    doc_ends = jnp.cumsum(lengths_row)
    places = jnp.arange(length, dtype=jnp.int32)
    return jnp.sum((places[:, None] >= doc_ends[None, :]).astype(jnp.int32), axis=1)


def conv_silu(pre_conv, seg_row, conv_w, conv_b):
    tap_count = conv_w.shape[0]
    row_len = pre_conv.shape[0]
    padded = jnp.pad(pre_conv, ((tap_count - 1, 0), (0, 0)))
    seg_pad = jnp.concatenate([jnp.full((tap_count - 1,), -1, jnp.int32), seg_row], axis=0)
    summed = conv_b[None, :] + conv_w[tap_count - 1][None, :] * pre_conv
    for offset in range(1, tap_count):
        start = tap_count - 1 - offset
        shifted = padded[start : start + row_len]
        same_doc = (seg_pad[start : start + row_len] == seg_row)[:, None]
        summed = summed + jnp.where(
            same_doc, conv_w[tap_count - 1 - offset][None, :] * shifted, 0.0
        )
    return jax.nn.silu(summed)


def block_step(a_neg, carried, inputs):
    states, prev_seg = carried
    x_block, b_block, c_block, dt_block, seg_block = inputs
    block_len = x_block.shape[0]
    log_rates = dt_block * a_neg[None, :]
    cumul = jnp.cumsum(log_rates, axis=0)
    cum_heads = cumul.T
    places = jnp.arange(block_len, dtype=jnp.int32)
    keep_mask = (places[:, None] > places[None, :]) & (seg_block[:, None] == seg_block[None, :])
    scores = jnp.dot(c_block, b_block.T, precision=highest)
    weighted = jnp.where(
        keep_mask[None],
        jnp.exp(jnp.minimum(cum_heads[:, :, None] - cum_heads[:, None, :], 0.0)) * scores[None],
        0.0,
    )
    inputs_dt = x_block * dt_block[:, :, None]
    y_inner = jnp.einsum("hts,shp->thp", weighted, inputs_dt, precision=highest)
    carried_in = jnp.where((seg_block == prev_seg)[:, None], jnp.exp(cumul), 0.0)
    y_carry = jnp.einsum("tn,hpn->thp", c_block, states, precision=highest) * carried_in[:, :, None]
    last_seg = seg_block[block_len - 1]
    tail_weights = jnp.where(
        (seg_block == last_seg)[:, None], jnp.exp(cumul[block_len - 1][None, :] - cumul), 0.0
    )
    carry_keep = jnp.where(last_seg == prev_seg, jnp.exp(cumul[block_len - 1]), 0.0)
    new_states = states * carry_keep[:, None, None] + jnp.einsum(
        "shp,sn->hpn", inputs_dt * tail_weights[:, :, None], b_block, precision=highest
    )
    return ((new_states, last_seg), y_inner + y_carry)


def scan_dir(x_row, b_row, c_row, dt_row, a_neg, seg_row):
    length = x_row.shape[0]
    block_count = length // BLOCK
    head_count = dt_row.shape[1]
    head_width = x_row.shape[1] // head_count
    state_width = b_row.shape[1]
    sliced = (
        x_row.reshape(block_count, BLOCK, head_count, head_width),
        b_row.reshape(block_count, BLOCK, state_width),
        c_row.reshape(block_count, BLOCK, state_width),
        dt_row.reshape(block_count, BLOCK, head_count),
        seg_row.reshape(block_count, BLOCK),
    )
    initial = (
        jnp.zeros((head_count, head_width, state_width), x_row.dtype),
        jnp.array(-1, jnp.int32),
    )
    advance = jax.checkpoint(partial(block_step, a_neg))
    final_carry, results = lax.scan(advance, initial, sliced)
    return (results.reshape(length, head_count * head_width), final_carry[0])


def rms_scale(values, gain):
    return (
        values
        * lax.rsqrt(jnp.mean(values * values, axis=1, keepdims=True) + epsilon)
        * gain[None, :]
    )


def gate_norm(mixed_vals, gate_vals, gain):
    gated = mixed_vals * jax.nn.silu(gate_vals)
    return (
        gated * lax.rsqrt(jnp.mean(gated * gated, axis=1, keepdims=True) + epsilon) * gain[None, :]
    )


def body(
    tokens,
    norm_gain,
    w_zx,
    w_bc,
    w_dt,
    conv_w,
    conv_b,
    dt_bias,
    a_log,
    d_skip,
    out_gain,
    w_out,
    doc_lengths,
    out_grad,
):
    direction = lax.axis_index("dir")
    forward_side = direction == 0
    full_zx, full_bc, full_dt, full_out = (
        lax.all_gather(w_zx, "dp", axis=0, tiled=True),
        lax.all_gather(w_bc, "dp", axis=0, tiled=True),
        lax.all_gather(w_dt, "dp", axis=0, tiled=True),
        lax.all_gather(w_out, "dp", axis=0, tiled=True),
    )
    row_count = tokens.shape[0]
    half_len = tokens.shape[1]
    token_count = row_count * half_len
    x_flat = tokens.reshape(token_count, D).astype(jnp.float32)
    normed_f, rms_pull = jax.vjp(rms_scale, x_flat, norm_gain)
    normed = normed_f.astype(jnp.bfloat16)
    zx_proj = jnp.dot(normed, full_zx, preferred_element_type=jnp.float32)
    bc_proj = jnp.dot(normed, full_bc, preferred_element_type=jnp.float32)
    dt_proj = jnp.dot(normed, full_dt, preferred_element_type=jnp.float32).astype(jnp.bfloat16)
    gate_z = zx_proj[:, :INNER]
    pre_conv = jnp.concatenate([zx_proj[:, INNER:], bc_proj], axis=1).astype(jnp.bfloat16)
    seg_rows = jax.vmap(partial(segment_ids, length=LEN))(doc_lengths)
    pre_rows = pre_conv.reshape(row_count, half_len, INNER + 2 * STATE)
    dt_rows = dt_proj.reshape(row_count, half_len, 2 * HEADS)
    rim_len = CONV - 1
    rim_in = shifted_2(pre_rows[:, half_len - rim_len :, :], "dir", 1)
    pre_ext = jnp.concatenate([rim_in, pre_rows], axis=1).astype(jnp.float32)
    seg_padded = jnp.concatenate([jnp.full((row_count, rim_len), -1, jnp.int32), seg_rows], axis=1)
    seg_ext = lax.dynamic_slice_in_dim(seg_padded, direction * half_len, half_len + rim_len, 1)
    seam_fwd = seg_rows[:, half_len - 1]
    seam_rev = seg_rows[:, half_len]

    def local_mixer(pre_vals, dt_vals, conv_w_in, conv_b_in, bias_in, alog_in, skip_in):
        a_fwd = -jnp.exp(alog_in[:HEADS])
        a_rev = -jnp.exp(alog_in[HEADS:])
        skip_cols = jnp.repeat(skip_in, HEADDIM)

        def one_half(row_args):
            pre_row, dt_row, seg_row, fwd_seam, rev_seam = row_args
            conv_out = conv_silu(pre_row, seg_row, conv_w_in, conv_b_in)[rim_len:]
            seg_here = seg_row[rim_len:]
            dt_fwd = jax.nn.softplus(dt_row[:, :HEADS] + bias_in[None, :HEADS])
            dt_rev = jax.nn.softplus(dt_row[:, HEADS:] + bias_in[None, HEADS:])
            x_in = conv_out[:, :INNER]
            b_in = conv_out[:, INNER : INNER + STATE]
            c_in = conv_out[:, INNER + STATE :]
            y_fwd, state_fwd = scan_dir(x_in, b_in, c_in, dt_fwd, a_fwd, seg_here)
            y_flip, state_rev = scan_dir(
                jnp.flip(x_in, axis=0),
                jnp.flip(b_in, axis=0),
                jnp.flip(c_in, axis=0),
                jnp.flip(dt_rev, axis=0),
                a_rev,
                jnp.flip(seg_here, axis=0),
            )
            y_local = y_fwd + jnp.flip(y_flip, axis=0) + x_in * skip_cols[None, :]
            sending = jnp.where(forward_side, state_fwd, state_rev)
            cum_fwd = jnp.cumsum(dt_fwd * a_fwd[None, :], axis=0)
            cum_rev = jnp.flip(
                jnp.cumsum(jnp.flip(dt_rev * a_rev[None, :], axis=0), axis=0), axis=0
            )
            carry_rev = jnp.where((seg_here == rev_seam)[:, None], jnp.exp(cum_rev), 0.0)
            carry_fwd = jnp.where((seg_here == fwd_seam)[:, None], jnp.exp(cum_fwd), 0.0)
            carry_weight = jnp.where(forward_side, carry_rev, carry_fwd)
            return (y_local, sending, c_in, carry_weight)

        return lax.map(one_half, (pre_vals, dt_vals, seg_ext, seam_fwd, seam_rev))

    local_parts, local_pull = jax.vjp(
        local_mixer, pre_ext, dt_rows.astype(jnp.float32), conv_w, conv_b, dt_bias, a_log, d_skip
    )
    y_local, sending, c_kept, carry_kept = local_parts
    received = partner(sending.astype(jnp.bfloat16), "dir", 0).astype(sending.dtype)

    def seam_term(state_in, c_vals, weights):
        term = (
            jnp.einsum("rtn,rhpn->rthp", c_vals, state_in, precision=highest)
            * weights[:, :, :, None]
        )
        return term.reshape(row_count, half_len, INNER)

    correction, seam_pull = jax.vjp(seam_term, received, c_kept, carry_kept)
    mixed = y_local + correction
    mixed_flat = mixed.reshape(token_count, INNER)
    normed_out_f, gate_pull = jax.vjp(gate_norm, mixed_flat, gate_z, out_gain)
    normed_out = normed_out_f.astype(jnp.bfloat16)
    summed_out = x_flat + jnp.dot(normed_out, full_out, preferred_element_type=jnp.float32)
    block_out = summed_out.astype(jnp.bfloat16).reshape(row_count, half_len, D)
    grad_flat = out_grad.reshape(token_count, D)
    grad_w_out = jnp.einsum("tk,td->kd", normed_out, grad_flat, preferred_element_type=jnp.float32)
    grad_normed_out = jnp.einsum(
        "td,kd->tk", grad_flat, full_out, preferred_element_type=jnp.float32
    )
    grad_mixed, grad_gate, grad_out_gain = gate_pull(grad_normed_out)
    grad_mixed_low = grad_mixed.astype(jnp.bfloat16).reshape(row_count, half_len, INNER)
    grad_mixed_vals = grad_mixed_low.astype(jnp.float32)
    grad_received, grad_c_seam, grad_carry = seam_pull(grad_mixed_vals)
    grad_sending = partner(grad_received.astype(jnp.bfloat16), "dir", 0).astype(grad_received.dtype)
    grad_ext, grad_dt_half, grad_conv_w, grad_conv_b, grad_dt_bias, grad_a_log, grad_d_skip = (
        local_pull((grad_mixed_vals, grad_sending, grad_c_seam, grad_carry))
    )
    rim_back = shifted_2(grad_ext[:, :rim_len, :], "dir", -1)
    grad_pre_half = grad_ext[:, rim_len:, :] + jnp.pad(
        rim_back, ((0, 0), (half_len - rim_len, 0), (0, 0))
    )
    grad_pre_flat = grad_pre_half.reshape(token_count, INNER + 2 * STATE)
    grad_zx = jnp.concatenate([grad_gate, grad_pre_flat[:, :INNER]], axis=1).astype(jnp.bfloat16)
    grad_bc = grad_pre_flat[:, INNER:].astype(jnp.bfloat16)
    grad_dt_low = grad_dt_half.reshape(token_count, 2 * HEADS).astype(jnp.bfloat16)
    grad_w_zx = jnp.einsum("tk,tj->kj", normed, grad_zx, preferred_element_type=jnp.float32)
    grad_w_bc = jnp.einsum("tk,tj->kj", normed, grad_bc, preferred_element_type=jnp.float32)
    grad_w_dt = jnp.einsum("tk,tj->kj", normed, grad_dt_low, preferred_element_type=jnp.float32)
    grad_normed = (
        jnp.einsum("tj,kj->tk", grad_zx, full_zx, preferred_element_type=jnp.float32)
        + jnp.einsum("tj,kj->tk", grad_bc, full_bc, preferred_element_type=jnp.float32)
        + jnp.einsum("tj,kj->tk", grad_dt_low, full_dt, preferred_element_type=jnp.float32)
    )
    grad_x_norm, grad_norm_gain = rms_pull(grad_normed)
    grad_tokens = (
        (grad_flat.astype(jnp.float32) + grad_x_norm)
        .astype(jnp.bfloat16)
        .reshape(row_count, half_len, D)
    )
    (
        sum_norm_gain,
        sum_w_zx,
        sum_w_bc,
        sum_w_dt,
        sum_conv_w,
        sum_conv_b,
        sum_dt_bias,
        sum_a_log,
        sum_d_skip,
        sum_out_gain,
        sum_w_out,
    ) = lax.psum(
        (
            grad_norm_gain,
            grad_w_zx,
            grad_w_bc,
            grad_w_dt,
            grad_conv_w,
            grad_conv_b,
            grad_dt_bias,
            grad_a_log,
            grad_d_skip,
            grad_out_gain,
            grad_w_out,
        ),
        ("dir", "dp"),
    )
    return (
        block_out,
        grad_tokens,
        sum_norm_gain,
        sum_w_zx,
        sum_w_bc,
        sum_w_dt,
        sum_conv_w,
        sum_conv_b,
        sum_dt_bias,
        sum_a_log,
        sum_d_skip,
        sum_out_gain,
        sum_w_out,
    )


def solution(mesh):
    placed = (
        P("dp", "dir", None),
        P(),
        P("dp", None),
        P("dp", None),
        P("dp", None),
        P(),
        P(),
        P(),
        P(),
        P(),
        P(),
        P("dp", None),
        P("dp", None),
        P("dp", "dir", None),
    )
    return jax.shard_map(
        body,
        mesh=mesh,
        in_specs=placed,
        out_specs=(
            P("dp", "dir", None),
            P("dp", "dir", None),
            P(),
            P(),
            P(),
            P(),
            P(),
            P(),
            P(),
            P(),
            P(),
            P(),
            P(),
        ),
        check_vma=False,
    )
```

profile of v0, /device:TPU:0, one launch (start us, length us, event | category | flops | bytes accessed | tf_op | source)
XLA Modules:
  0.0 1082.4 jit_solution(1993637158967317221)
XLA Ops:
  10.2 24.4 %all_gather.14 = bf16[768,128]{1,0:T(8,128)(2,1)S(1)} all-gather(bf16[48,128]{1,0:T(8,128)(2,1)} %param.28), channel_id=1, replica_groups=mesh['dir'=2,'dp'=16] {'dp'}, dimensions={0}, use_global_device_ids=true | all-gather | bytes 208896 | tf_op jit(solution)/shard_map/all_gather | solution.py:138
  37.3 18.9 %all_gather.12 = bf16[768,48]{1,0:T(8,128)(2,1)S(1)} all-gather(bf16[48,48]{1,0:T(8,128)(2,1)} %param.29), channel_id=1, replica_groups=mesh['dir'=2,'dp'=16] {'dp'}, dimensions={0}, use_global_device_ids=true | all-gather | bytes 78336 | tf_op jit(solution)/shard_map/all_gather | solution.py:139
  67.4 4.6 fusion.288
  84.9 4.9 fusion.204
  93.8 24.7 %rev.107 = f32[512,1536]{1,0:T(8,128)} reverse(f32[512,1536]{1,0:T(8,128)} %slice.328), dimensions={0} | reverse | bytes 6291456 | tf_op jit(solution)/shard_map/jvp()/while/body/eval_jaxpr/jit(_flip)/rev | solution.py:180
  118.5 5.5 reshape.1386
  124.5 5.5 reshape.1387
  129.9 6.1 copy.490
  140.6 59.0 %while.230 = (s32[]{:T(128)}, f32[24,64,64]{2,1,0:T(8,128)S(1)}, s32[]{:T(128)}, f32[4,128,24,64]{1,3,2,0:T(8,128)}, f32[4,24,64,64]{3,2,1,0:T(8,128)}, /*index=...) while((s32[]{:T(128)}, f32[24,64,64]{2,1,0:T(8,128)S(1)}, ...), condition=%wide.region_8.10_spmd.clone, body=%wide.region_6.9_spmd.clone.sunk | while | flops 620061952 | bytes 7651091 | solution.py:99
  202.6 6.2 copy.484
  213.5 63.2 %while.229 = (s32[]{:T(128)}, f32[24,64,64]{2,1,0:T(8,128)S(1)}, s32[]{:T(128)}, f32[4,128,24,64]{1,3,2,0:T(8,128)}, f32[4,24,64,64]{3,2,1,0:T(8,128)}, /*index=...) while((s32[]{:T(128)}, f32[24,64,64]{2,1,0:T(8,128)S(1)}, ...), condition=%wide.region_5.7_spmd.clone, body=%wide.region_3.6_spmd.clone.sunk | while | flops 620061952 | bytes 7257875 | solution.py:99
  280.4 5.9 copy.544
  286.3 4.7 reshape.1381
  291.0 15.7 %rev.110 = f32[512,1536]{1,0:T(8,128)} reverse(f32[512,1536]{1,0:T(8,128)S(1)} %reshape.1381), dimensions={0} | reverse | bytes 6291456 | tf_op jit(solution)/shard_map/jvp()/while/body/eval_jaxpr/jit(_flip)/rev | solution.py:187
  306.7 5.9 copy.543
  312.6 6.3 reshape.1380
  318.9 5.2 broadcast_multiply_fusion.4
  327.7 7.1 multiply_reduce_fusion.16
  340.2 5.0 multiply_reduce_fusion.12
  345.7 5.7 multiply_reduce_fusion.13
  361.0 5.5 fusion.230
  371.7 5.0 reduce-window.64
  380.5 15.9 %reverse.3 = f32[512,1536]{1,0:T(8,128)} reverse(bf16[512,1536]{1,0:T(8,128)(2,1)S(1)} %get-tuple-element.2333), dimensions={0} | reverse | bytes 4718592 | tf_op jit(solution)/shard_map/reverse
  396.4 6.2 copy.519
  404.1 5.0 reduce-window.66
  413.3 6.1 copy.511
  424.7 144.4 %while.232 = (s32[]{:T(128)}, f32[24]{0:T(128)}, f32[24,64,64]{2,1,0:T(8,128)S(1)}, f32[4,128,24,64]{1,3,2,0:T(8,128)}, f32[4,128,64]{1,2,0:T(8,128)}, /*index=5...) while((s32[]{:T(128)}, f32[24]{0:T(128)}, ...), condition=%wide.region_40.42_spmd.clone, body=%wide.region_28.41_spmd.clone.sunk | while | flops 1408011520 | bytes 22274224 | solution.py:99
  438.4 4.8 multiply_reduce_fusion.28
  444.2 4.7 fusion.494
  474.4 4.8 multiply_reduce_fusion.28
  480.2 4.7 fusion.494
  510.3 4.8 multiply_reduce_fusion.28
  516.2 4.7 fusion.494
  546.3 4.8 multiply_reduce_fusion.28
  552.1 4.7 fusion.494
  574.8 142.2 %while.231 = (s32[]{:T(128)}, f32[24]{0:T(128)}, f32[24,64,64]{2,1,0:T(8,128)S(1)}, f32[4,128,24,64]{1,3,2,0:T(8,128)}, f32[4,128,64]{1,2,0:T(8,128)}, /*index=5...) while((s32[]{:T(128)}, f32[24]{0:T(128)}, ...), condition=%wide.region_27.29_spmd.clone, body=%wide.region_15.28_spmd.clone.sunk | while | flops 1408011520 | bytes 19111204 | solution.py:99
  588.5 4.5 multiply_reduce_fusion.25
  624.0 4.5 multiply_reduce_fusion.25
  725.9 5.8 copy.553
  731.7 6.3 reshape.1385
  742.0 6.2 reshape.1384
  748.2 24.7 %rev.115 = f32[512,1536]{1,0:T(8,128)} reverse(f32[512,1536]{1,0:T(8,128)} %reshape.1384), dimensions={0} | reverse | bytes 6291456 | tf_op jit(solution)/shard_map/transpose(jvp())/while/body/eval_jaxpr/jit(_flip)/rev | solution.py:180
  783.2 5.5 multiply_reduce_fusion.11
  800.1 5.6 fusion.210
  814.2 5.6 fusion.221
  819.8 42.1 %all-reduce.25 = (f32[768]{0:T(1024)}, f32[4,1664]{1,0:T(4,128)}, f32[1664]{0:T(1024)}, f32[48]{0:T(128)}, f32[48]{0:T(128)}, /*index=5*/f32[24]{0:T(128)}, f32[1536]{0:T(1024)}) all-reduce(f32[768]{0:T(1024)S(1)} %get-tuple-element.2195, f32[4,1664]{1,0:T(4,128)S(1)} %pad_add_fusion.3, ...), channel_id=1, replica_groups=mesh['dir'=2,'dp'=16] {'dir','dp'}, use_global_device_ids=true, to_apply=%region_48.50 | all-reduce | flops 10744 | bytes 85952 | tf_op jit(solution)/shard_map/psum | solution.py:267
  863.3 199.8 %all-reduce.29.cloned.1.call-done = (f32[768,3072]{1,0:T(8,128)}, f32[768,128]{1,0:T(8,128)}, f32[768,48]{0,1:T(8,128)}, f32[1536,768]{1,0:T(8,128)}) async-done(((f32[768,3072]{1,0:T(8,128)}, f32[768,128]{1,0:T(8,128)}, f32[768,48]{0,1:T(8,128)}, f32[1536,768]{1,0:T(8,128)}), (f32[768,3072]{1,0:T(8,128)}, f32[768,128]{1,0:T(8,128)}, f32[768,48]{0,1:T(8,128)}, ...) | async-done | bytes 14696464 | tf_op jit(solution)/shard_map/psum | solution.py:267
  1063.1 8.8 copy.749
  (959 shorter events, 479.6 us)
Async XLA Ops:
  7.2 50.6 %copy-start.20 = (bf16[1,512,768]{2,1,0:T(8,128)(2,1)S(1)}, bf16[1,512,768]{2,1,0:T(8,128)(2,1)}, u32[]{:S(2)}) copy-start(bf16[1,512,768]{2,1,0:T(8,128)(2,1)} %param.25) | copy-start | bytes 2359300
  7.2 50.6 %copy-start.65 = (f32[768]{0:T(1024)S(1)}, f32[768]{0:T(1024)}, u32[]{:S(2)}) copy-start(f32[768]{0:T(1024)} %param.26) | copy-start | bytes 9220
  7.2 51.2 %copy-start.120 = (f32[48]{0:T(128)S(1)}, f32[48]{0:T(128)}, u32[]{:S(2)}) copy-start(f32[48]{0:T(128)} %param.32) | copy-start | bytes 580
  7.2 51.2 %copy-start.112 = (f32[48]{0:T(128)S(1)}, f32[48]{0:T(128)}, u32[]{:S(2)}) copy-start(f32[48]{0:T(128)} %param.33) | copy-start | bytes 580
  7.2 60.2 %all-gather.3.cloned.1.call-start = ((), (), s32[]{:S(2)}) async-start(), calls=%async_computation | async-start | bytes 5013504 | tf_op jit(solution)/shard_map/all_gather | solution.py:137
  8.0 332.2 %all-gather.5.cloned.1.call-start = ((), (), s32[]{:S(2)}) async-start(), calls=%async_computation.1 | async-start | bytes 2506752 | tf_op jit(solution)/shard_map/all_gather | solution.py:140
  8.7 1054.4 %all-reduce.29.cloned.1.call-start = ((), (), s32[]{:S(2)}) async-start(), calls=%async_computation.2 | async-start | bytes 29392896 | tf_op jit(solution)/shard_map/psum | solution.py:267
  10.1 48.9 %copy-start.97 = (f32[512]{0:T(512)}, f32[512]{0:T(512)S(1)}, u32[]{:S(2)}) copy-start(f32[512]{0:T(512)S(1)} %fusion.222) | copy-start | bytes 6148
  10.1 61.9 %copy-start.70 = (f32[512]{0:T(512)}, f32[512]{0:T(512)S(1)}, u32[]{:S(2)}) copy-start(f32[512]{0:T(512)S(1)} %fusion.273) | copy-start | bytes 6148
  34.6 37.5 %copy-start.47 = (bf16[768,128]{1,0:T(8,128)(2,1)}, bf16[768,128]{1,0:T(8,128)(2,1)S(1)}, u32[]{:S(2)}) copy-start(bf16[768,128]{1,0:T(8,128)(2,1)S(1)} %all_gather.14) | copy-start | bytes 589828
  36.2 48.7 %copy-start.105 = (pred[515]{0:T(1024)(128)(4,1)}, pred[515]{0:T(1024)(128)(4,1)S(1)}, u32[]{:S(2)}) copy-start(pred[515]{0:T(1024)(128)(4,1)S(1)} %get-tuple-element.2392) | copy-start | bytes 1549
  36.2 48.7 %copy-start.107 = (pred[515]{0:T(1024)(128)(4,1)}, pred[515]{0:T(1024)(128)(4,1)S(1)}, u32[]{:S(2)}) copy-start(pred[515]{0:T(1024)(128)(4,1)S(1)} %get-tuple-element.2393) | copy-start | bytes 1549
  36.2 48.7 %copy-start.109 = (pred[515]{0:T(1024)(128)(4,1)}, pred[515]{0:T(1024)(128)(4,1)S(1)}, u32[]{:S(2)}) copy-start(pred[515]{0:T(1024)(128)(4,1)S(1)} %get-tuple-element.2394) | copy-start | bytes 1549
  37.2 47.7 %copy-start.80 = (f32[1664]{0:T(1024)}, f32[1664]{0:T(1024)S(1)}, u32[]{:S(2)}) copy-start(f32[1664]{0:T(1024)S(1)} %get-tuple-element.2197) | copy-start | bytes 19972
  37.2 47.7 %copy-start.82 = (f32[1664]{0:T(1024)}, f32[1664]{0:T(1024)S(1)}, u32[]{:S(2)}) copy-start(f32[1664]{0:T(1024)S(1)} %get-tuple-element.2198) | copy-start | bytes 19972
  37.2 47.7 %copy-start.84 = (f32[1664]{0:T(1024)}, f32[1664]{0:T(1024)S(1)}, u32[]{:S(2)}) copy-start(f32[1664]{0:T(1024)S(1)} %get-tuple-element.2199) | copy-start | bytes 19972
  37.2 47.7 %copy-start.86 = (f32[1664]{0:T(1024)}, f32[1664]{0:T(1024)S(1)}, u32[]{:S(2)}) copy-start(f32[1664]{0:T(1024)S(1)} %get-tuple-element.2200) | copy-start | bytes 19972
  56.2 15.8 %copy-start.49 = (bf16[768,48]{1,0:T(8,128)(2,1)}, bf16[768,48]{1,0:T(8,128)(2,1)S(1)}, u32[]{:S(2)}) copy-start(bf16[768,48]{1,0:T(8,128)(2,1)S(1)} %all_gather.12) | copy-start | bytes 221188
  57.8 25.9 %copy-start.42 = (bf16[512,128]{1,0:T(8,128)(2,1)}, bf16[512,128]{1,0:T(8,128)(2,1)S(1)}, u32[]{:S(2)}) copy-start(bf16[512,128]{1,0:T(8,128)(2,1)S(1)} %convolution_convert_fusion.1) | copy-start | bytes 393220
  59.0 13.1 %copy-start.118 = (f32[24]{0:T(128)}, f32[24]{0:T(128)S(1)}, u32[]{:S(2)}) copy-start(f32[24]{0:T(128)S(1)} %get-tuple-element.2410) | copy-start | bytes 292
  59.8 19.6 %copy-start.56 = (f32[512,24]{0,1:T(8,128)}, f32[512,24]{0,1:T(8,128)S(1)}, u32[]{:S(2)}) copy-start(f32[512,24]{0,1:T(8,128)S(1)} %get-tuple-element.2343) | copy-start | bytes 147460
  59.8 20.1 %copy-start.52 = (f32[512,24]{0,1:T(8,128)}, f32[512,24]{0,1:T(8,128)S(1)}, u32[]{:S(2)}) copy-start(f32[512,24]{0,1:T(8,128)S(1)} %get-tuple-element.2387) | copy-start | bytes 147460
  75.0 8.7 collective-permute-start
  81.6 246.0 %copy-start.78 = (f32[1536]{0:T(1024)}, f32[1536]{0:T(1024)S(1)}, u32[]{:S(2)}) copy-start(f32[1536]{0:T(1024)S(1)} %mul.1288) | copy-start | bytes 18436
  91.7 32.3 %copy-start.37 = (f32[512,64]{1,0:T(8,128)}, f32[512,64]{1,0:T(8,128)S(1)}, u32[]{:S(2)}) copy-start(f32[512,64]{1,0:T(8,128)S(1)} %get-tuple-element.2379) | copy-start | bytes 393220
  91.7 32.5 %copy-start.36 = (f32[512,64]{1,0:T(8,128)}, f32[512,64]{1,0:T(8,128)S(1)}, u32[]{:S(2)}) copy-start(f32[512,64]{1,0:T(8,128)S(1)} %get-tuple-element.2378) | copy-start | bytes 393220
  199.6 9.2 copy-start.28
  199.6 9.1 copy-start.33
  199.6 9.1 copy-start.34
  213.5 64.1 %copy-start.54 = (f32[512,24]{0,1:T(8,128)S(1)}, f32[512,24]{0,1:T(8,128)}, u32[]{:S(2)}) copy-start(f32[512,24]{0,1:T(8,128)} %rev.112) | copy-start | bytes 147460
  277.6 41.4 %collective-permute-start.1 = (bf16[1,24,64,64]{3,2,1,0:T(8,128)(2,1)}, bf16[1,24,64,64]{3,2,1,0:T(8,128)(2,1)}, u32[]{:S(2)}, u32[]{:S(2)}) collective-permute-start(bf16[1,24,64,64]{3,2,1,0:T(8,128)(2,1)} %fusion.246), channel_id=1, source_target_pairs={{0,16},{16,0},{1,17},{17,1},{2,18},{18,2},{3,19},{19,3},{4,20},{20... | collective-permute-start | bytes 589832 | tf_op jit(solution)/shard_map/ppermute | solution.py:26
  327.7 8.8 copy-start.30
  327.7 8.8 copy-start.76
  334.8 10.4 copy-start.94
  351.4 29.1 %copy-start.1 = (bf16[512,1536]{1,0:T(8,128)(2,1)}, bf16[512,1536]{1,0:T(8,128)(2,1)S(1)}, u32[]{:S(2)}) copy-start(bf16[512,1536]{1,0:T(8,128)(2,1)S(1)} %get-tuple-element.2333) | copy-start | bytes 4718596
  366.5 52.9 %collective-permute-start.2 = (bf16[1,24,64,64]{3,2,1,0:T(8,128)(2,1)}, bf16[1,24,64,64]{3,2,1,0:T(8,128)(2,1)}, u32[]{:S(2)}, u32[]{:S(2)}) collective-permute-start(bf16[1,24,64,64]{3,2,1,0:T(8,128)(2,1)} %fusion.230), channel_id=1, source_target_pairs={{0,16},{16,0},{1,17},{17,1},{2,18},{18,2},{3,19},{19,3},{4,20},{20... | collective-permute-start | bytes 589832 | tf_op jit(solution)/shard_map/ppermute | solution.py:26
  396.4 13.4 %copy-start.17 = (f32[512,1536]{1,0:T(8,128)S(1)}, f32[512,1536]{1,0:T(8,128)}, u32[]{:S(2)}) copy-start(f32[512,1536]{1,0:T(8,128)} %reverse.3) | copy-start | bytes 9437188
  748.2 24.7 %copy-start.45 = (f32[4,128,64]{2,1,0:T(8,128)S(1)}, f32[4,128,64]{2,1,0:T(8,128)}, u32[]{:S(2)}) copy-start(f32[4,128,64]{2,1,0:T(8,128)} %copy.522) | copy-start | bytes 393220
  748.2 24.7 %copy-start.46 = (f32[512,64]{1,0:T(8,128)S(1)}, f32[512,64]{1,0:T(8,128)}, u32[]{:S(2)}) copy-start(f32[512,64]{1,0:T(8,128)} %rev.114) | copy-start | bytes 393220
  748.2 24.7 %copy-start.2 = (bf16[512,1536]{1,0:T(8,128)(2,1)S(1)}, bf16[512,1536]{1,0:T(8,128)(2,1)}, u32[]{:S(2)}) copy-start(bf16[512,1536]{1,0:T(8,128)(2,1)} %copy-done.1) | copy-start | bytes 4718596
  748.2 24.7 %copy-start.79 = (f32[1536]{0:T(1024)S(1)}, f32[1536]{0:T(1024)}, u32[]{:S(2)}) copy-start(f32[1536]{0:T(1024)} %copy-done.78) | copy-start | bytes 18436
  791.5 5.7 collective-permute-start.3
  814.2 47.7 %copy-start.98 = (f32[512]{0:T(512)S(1)}, f32[512]{0:T(512)}, u32[]{:S(2)}) copy-start(f32[512]{0:T(512)} %copy-done.97) | copy-start | bytes 6148
  814.2 47.7 %copy-start.32 = (bf16[1,512,768]{2,1,0:T(8,128)(2,1)S(1)}, bf16[1,512,768]{2,1,0:T(8,128)(2,1)}, u32[]{:S(2)}) copy-start(bf16[1,512,768]{2,1,0:T(8,128)(2,1)} %param.38) | copy-start | bytes 2359300
  1063.1 10.2 slice-start
  1063.1 8.8 copy-start.60
  1063.1 9.5 copy-start.69
  1063.1 10.2 slice-start.1
  (134 other events, 619.7 us)
Sparse Core Ops, SparseCore 0:
  10.3 57.0 all-gather.2
  69.7 41.3 all-gather.4
  805.8 257.2 all-reduce.28
where the time goes:
time: 1100 us; the launch traced here: 1080 us
  local copies, waits for them, and re-layouts  336 us (31%)
  matrix products  265 us (24%)
  waiting for transfers between devices  207 us (19%)
  other arithmetic  142 us (13%)
  blocking collectives  85.5 us (8%)
  loops' own time  24 us (2%)
  between operations  15.6 us (1%)
    psum x1, waiting for transfers between devices, body(): lax.psum((grad_norm_gain, grad_w_zx, grad_w_bc, grad_w_dt, grad_conv_w, g...  200 us
    dot_general x24, matrix products, block_step(): y_inner = jnp.einsum('hts,shp->thp', weighted, inputs_dt, precision=highest)  108 us
    unnamed x228, local copies, waits for them, and re-layouts  52.9 us
    rev x2, local copies, waits for them, and re-layouts, one_half(): jnp.flip(x_in, axis=0)  49.4 us
    dot_general x32, matrix products, block_step(): jnp.einsum('tn,hpn->thp', c_block, states, precision=highest)  48.6 us
    dot_general x24, matrix products, block_step(): jnp.einsum('shp,sn->hpn', inputs_dt * tail_weights[:, :, None], b_block,...  48.2 us
    psum x1, blocking collectives, body(): lax.psum((grad_norm_gain, grad_w_zx, grad_w_bc, grad_w_dt, grad_conv_w, g...  42.1 us
    squeeze x48, local copies, waits for them, and re-layouts, scan_dir(): final_carry, results = lax.scan(advance, initial, sliced)  41.2 us
  transfers between devices with their start and end apart: 7, of which 3 were waited for; matrix products, arithmetic and copies ran while one was open for 30% of the time, Pallas kernels for 0%

commit v1 on v0

--- a/solution.py
+++ b/solution.py
@@ -265,20 +265,23 @@
         sum_out_gain,
         sum_w_out,
     ) = lax.psum(
-        (
-            grad_norm_gain,
-            grad_w_zx,
-            grad_w_bc,
-            grad_w_dt,
-            grad_conv_w,
-            grad_conv_b,
-            grad_dt_bias,
-            grad_a_log,
-            grad_d_skip,
-            grad_out_gain,
-            grad_w_out,
+        lax.psum(
+            (
+                grad_norm_gain,
+                grad_w_zx,
+                grad_w_bc,
+                grad_w_dt,
+                grad_conv_w,
+                grad_conv_b,
+                grad_dt_bias,
+                grad_a_log,
+                grad_d_skip,
+                grad_out_gain,
+                grad_w_out,
+            ),
+            "dp",
         ),
-        ("dir", "dp"),
+        "dir",
     )
     return (
         block_out,

time: 1100 us -> 1440 us (1.31)
  waiting for transfers between devices: 207 us -> 526 us
  blocking collectives: 85.5 us -> 114 us
    psum x0 -> x1, waiting for transfers between devices: none -> 252 us  [body(): lax.psum(lax.psum((grad_norm_gain, grad_w_zx, grad_w_bc, grad_w_dt, grad_...]
    psum x1, waiting for transfers between devices: 200 us -> 266 us  [body(): lax.psum((grad_norm_gain, grad_w_zx, grad_w_bc, grad_w_dt, grad_conv_w, g...]
    psum x1, blocking collectives: 42.1 us -> 60.9 us  [body(): lax.psum((grad_norm_gain, grad_w_zx, grad_w_bc, grad_w_dt, grad_conv_w, g...]
  transfers between devices with their start and end apart: 7 -> 8, of which waited for: 3 -> 4; matrix products, arithmetic and copies ran while one was open for 30% -> 23% of each run, Pallas kernels for 0% -> 0%
where the time goes in v1:
time: 1440 us; the launch traced here: 1430 us
  waiting for transfers between devices  526 us (37%)
  local copies, waits for them, and re-layouts  335 us (23%)
  matrix products  266 us (18%)
  other arithmetic  142 us (10%)
  blocking collectives  114 us (8%)
  loops' own time  24 us (2%)
  between operations  15.7 us (1%)
    psum x1, waiting for transfers between devices, body(): lax.psum((grad_norm_gain, grad_w_zx, grad_w_bc, grad_w_dt, grad_conv_w, g...  266 us
    psum x1, waiting for transfers between devices, body(): lax.psum(lax.psum((grad_norm_gain, grad_w_zx, grad_w_bc, grad_w_dt, grad_...  252 us
    dot_general x24, matrix products, block_step(): y_inner = jnp.einsum('hts,shp->thp', weighted, inputs_dt, precision=highest)  108 us
    psum x1, blocking collectives, body(): lax.psum((grad_norm_gain, grad_w_zx, grad_w_bc, grad_w_dt, grad_conv_w, g...  60.9 us
    unnamed x228, local copies, waits for them, and re-layouts  52.9 us
    rev x2, local copies, waits for them, and re-layouts, one_half(): jnp.flip(x_in, axis=0)  49.4 us
    dot_general x32, matrix products, block_step(): jnp.einsum('tn,hpn->thp', c_block, states, precision=highest)  48.5 us
    dot_general x24, matrix products, block_step(): jnp.einsum('shp,sn->hpn', inputs_dt * tail_weights[:, :, None], b_block,...  48.2 us
  transfers between devices with their start and end apart: 8, of which 4 were waited for; matrix products, arithmetic and copies ran while one was open for 23% of the time, Pallas kernels for 0%

profile of v1, /device:TPU:0, one launch (start us, length us, event | category | flops | bytes accessed | tf_op | source)
XLA Modules:
  0.0 1429.1 jit_solution(1252789076566670540)
XLA Ops:
  10.2 24.4 %all_gather.14 = bf16[768,128]{1,0:T(8,128)(2,1)S(1)} all-gather(bf16[48,128]{1,0:T(8,128)(2,1)} %param.28), channel_id=1, replica_groups=mesh['dir'=2,'dp'=16] {'dp'}, dimensions={0}, use_global_device_ids=true | all-gather | bytes 208896 | tf_op jit(solution)/shard_map/all_gather | solution.py:138
  37.3 18.9 %all_gather.12 = bf16[768,48]{1,0:T(8,128)(2,1)S(1)} all-gather(bf16[48,48]{1,0:T(8,128)(2,1)} %param.29), channel_id=1, replica_groups=mesh['dir'=2,'dp'=16] {'dp'}, dimensions={0}, use_global_device_ids=true | all-gather | bytes 78336 | tf_op jit(solution)/shard_map/all_gather | solution.py:139
  67.4 4.6 fusion.288
  84.9 4.8 fusion.204
  93.7 24.7 %rev.107 = f32[512,1536]{1,0:T(8,128)} reverse(f32[512,1536]{1,0:T(8,128)} %slice.328), dimensions={0} | reverse | bytes 6291456 | tf_op jit(solution)/shard_map/jvp()/while/body/eval_jaxpr/jit(_flip)/rev | solution.py:180
  118.4 5.5 reshape.1386
  124.4 5.5 reshape.1387
  129.8 6.1 copy.490
  140.5 58.7 %while.230 = (s32[]{:T(128)}, f32[24,64,64]{2,1,0:T(8,128)S(1)}, s32[]{:T(128)}, f32[4,128,24,64]{1,3,2,0:T(8,128)}, f32[4,24,64,64]{3,2,1,0:T(8,128)}, /*index=...) while((s32[]{:T(128)}, f32[24,64,64]{2,1,0:T(8,128)S(1)}, ...), condition=%wide.region_8.10_spmd.clone, body=%wide.region_6.9_spmd.clone.sunk | while | flops 620061952 | bytes 7651091 | solution.py:99
  202.2 6.2 copy.484
  213.0 63.1 %while.229 = (s32[]{:T(128)}, f32[24,64,64]{2,1,0:T(8,128)S(1)}, s32[]{:T(128)}, f32[4,128,24,64]{1,3,2,0:T(8,128)}, f32[4,24,64,64]{3,2,1,0:T(8,128)}, /*index=...) while((s32[]{:T(128)}, f32[24,64,64]{2,1,0:T(8,128)S(1)}, ...), condition=%wide.region_5.7_spmd.clone, body=%wide.region_3.6_spmd.clone.sunk | while | flops 620061952 | bytes 7257875 | solution.py:99
  279.9 5.9 copy.544
  285.8 4.7 reshape.1381
  290.5 15.7 %rev.110 = f32[512,1536]{1,0:T(8,128)} reverse(f32[512,1536]{1,0:T(8,128)S(1)} %reshape.1381), dimensions={0} | reverse | bytes 6291456 | tf_op jit(solution)/shard_map/jvp()/while/body/eval_jaxpr/jit(_flip)/rev | solution.py:187
  306.2 5.9 copy.543
  312.1 6.3 reshape.1380
  318.4 5.2 broadcast_multiply_fusion.4
  327.2 7.1 multiply_reduce_fusion.16
  339.7 5.0 multiply_reduce_fusion.12
  345.2 5.7 multiply_reduce_fusion.13
  360.6 5.5 fusion.230
  371.2 5.0 reduce-window.64
  380.0 15.9 %reverse.3 = f32[512,1536]{1,0:T(8,128)} reverse(bf16[512,1536]{1,0:T(8,128)(2,1)S(1)} %get-tuple-element.2344), dimensions={0} | reverse | bytes 4718592 | tf_op jit(solution)/shard_map/reverse
  395.9 6.3 copy.519
  403.7 5.0 reduce-window.66
  412.8 6.1 copy.511
  424.3 143.7 %while.232 = (s32[]{:T(128)}, f32[24]{0:T(128)}, f32[24,64,64]{2,1,0:T(8,128)S(1)}, f32[4,128,24,64]{1,3,2,0:T(8,128)}, f32[4,128,64]{1,2,0:T(8,128)}, /*index=5...) while((s32[]{:T(128)}, f32[24]{0:T(128)}, ...), condition=%wide.region_40.42_spmd.clone, body=%wide.region_28.41_spmd.clone.sunk | while | flops 1408011520 | bytes 22274224 | solution.py:99
  438.0 4.8 multiply_reduce_fusion.28
  443.8 4.7 fusion.494
  473.8 4.8 multiply_reduce_fusion.28
  479.6 4.7 fusion.494
  509.6 4.8 multiply_reduce_fusion.28
  515.4 4.7 fusion.494
  545.3 4.8 multiply_reduce_fusion.28
  551.2 4.7 fusion.494
  573.8 142.0 %while.231 = (s32[]{:T(128)}, f32[24]{0:T(128)}, f32[24,64,64]{2,1,0:T(8,128)S(1)}, f32[4,128,24,64]{1,3,2,0:T(8,128)}, f32[4,128,64]{1,2,0:T(8,128)}, /*index=5...) while((s32[]{:T(128)}, f32[24]{0:T(128)}, ...), condition=%wide.region_27.29_spmd.clone, body=%wide.region_15.28_spmd.clone.sunk | while | flops 1408011520 | bytes 19111204 | solution.py:99
  724.7 5.8 copy.553
  730.5 6.3 reshape.1385
  740.8 6.2 reshape.1384
  747.0 24.7 %rev.115 = f32[512,1536]{1,0:T(8,128)} reverse(f32[512,1536]{1,0:T(8,128)} %reshape.1384), dimensions={0} | reverse | bytes 6291456 | tf_op jit(solution)/shard_map/transpose(jvp())/while/body/eval_jaxpr/jit(_flip)/rev | solution.py:180
  782.0 5.5 multiply_reduce_fusion.11
  798.8 5.6 fusion.210
  804.5 266.0 %all-reduce.32.cloned.1.call-done = (f32[768,3072]{1,0:T(8,128)}, f32[768,128]{1,0:T(8,128)}, f32[768,48]{0,1:T(8,128)}, f32[1536,768]{1,0:T(8,128)}) async-done(((f32[768,3072]{1,0:T(8,128)}, f32[768,128]{1,0:T(8,128)}, f32[768,48]{0,1:T(8,128)}, f32[1536,768]{1,0:T(8,128)}), (f32[768,3072]{1,0:T(8,128)}, f32[768,128]{1,0:T(8,128)}, f32[768,48]{0,1:T(8,128)}, ...) | async-done | bytes 14696464 | tf_op jit(solution)/shard_map/psum | solution.py:268
  1079.0 5.8 fusion.221
  1084.8 60.9 %all-reduce.25 = (f32[768]{0:T(1024)S(1)}, f32[4,1664]{1,0:T(4,128)S(1)}, f32[1664]{0:T(1024)S(1)}, f32[48]{0:T(128)S(1)}, f32[48]{0:T(128)S(1)}, /*index=5*/f32[24]{0:T(128)S(1)}, f32[1536]{0:T(1024)S(1)}) all-reduce(f32[768]{0:T(1024)S(1)} %get-tuple-element.2195, ...), channel_id=1, replica_groups=mesh['dir'=2,'dp'=16] {'dp'}, use_global_device_ids=true, to_apply=%region_48.50 | all-reduce | flops 10744 | bytes 85952 | tf_op jit(solution)/shard_map/psum | solution.py:268
  1145.8 10.2 all-reduce.27
  1157.3 252.4 %all-reduce.34.cloned.1.call-done = (f32[768,3072]{1,0:T(8,128)}, f32[768,128]{1,0:T(8,128)}, f32[768,48]{0,1:T(8,128)}, f32[1536,768]{1,0:T(8,128)}) async-done(((f32[768,3072]{1,0:T(8,128)}, f32[768,128]{1,0:T(8,128)}, f32[768,48]{0,1:T(8,128)}, f32[1536,768]{1,0:T(8,128)}), (f32[768,3072]{1,0:T(8,128)}, f32[768,128]{1,0:T(8,128)}, f32[768,48]{0,1:T(8,128)}, ...) | async-done | bytes 14696464 | tf_op jit(solution)/shard_map/psum | solution.py:267
  1409.8 8.8 copy.753
  (963 shorter events, 487.3 us)
Async XLA Ops:
  7.2 50.6 %copy-start.20 = (bf16[1,512,768]{2,1,0:T(8,128)(2,1)S(1)}, bf16[1,512,768]{2,1,0:T(8,128)(2,1)}, u32[]{:S(2)}) copy-start(bf16[1,512,768]{2,1,0:T(8,128)(2,1)} %param.25) | copy-start | bytes 2359300
  7.2 50.6 %copy-start.65 = (f32[768]{0:T(1024)S(1)}, f32[768]{0:T(1024)}, u32[]{:S(2)}) copy-start(f32[768]{0:T(1024)} %param.26) | copy-start | bytes 9220
  7.2 51.2 %copy-start.120 = (f32[48]{0:T(128)S(1)}, f32[48]{0:T(128)}, u32[]{:S(2)}) copy-start(f32[48]{0:T(128)} %param.32) | copy-start | bytes 580
  7.2 51.2 %copy-start.112 = (f32[48]{0:T(128)S(1)}, f32[48]{0:T(128)}, u32[]{:S(2)}) copy-start(f32[48]{0:T(128)} %param.33) | copy-start | bytes 580
  7.2 60.2 %all-gather.3.cloned.1.call-start = ((), (), s32[]{:S(2)}) async-start(), calls=%async_computation | async-start | bytes 5013504 | tf_op jit(solution)/shard_map/all_gather | solution.py:137
  8.0 331.7 %all-gather.5.cloned.1.call-start = ((), (), s32[]{:S(2)}) async-start(), calls=%async_computation.1 | async-start | bytes 2506752 | tf_op jit(solution)/shard_map/all_gather | solution.py:140
  8.7 1061.8 %all-reduce.32.cloned.1.call-start = ((), (), s32[]{:S(2)}) async-start(), calls=%async_computation.2 | async-start | bytes 29392896 | tf_op jit(solution)/shard_map/psum | solution.py:268
  10.1 48.9 %copy-start.97 = (f32[512]{0:T(512)}, f32[512]{0:T(512)S(1)}, u32[]{:S(2)}) copy-start(f32[512]{0:T(512)S(1)} %fusion.222) | copy-start | bytes 6148
  10.1 61.9 %copy-start.70 = (f32[512]{0:T(512)}, f32[512]{0:T(512)S(1)}, u32[]{:S(2)}) copy-start(f32[512]{0:T(512)S(1)} %fusion.273) | copy-start | bytes 6148
  34.6 37.5 %copy-start.47 = (bf16[768,128]{1,0:T(8,128)(2,1)}, bf16[768,128]{1,0:T(8,128)(2,1)S(1)}, u32[]{:S(2)}) copy-start(bf16[768,128]{1,0:T(8,128)(2,1)S(1)} %all_gather.14) | copy-start | bytes 589828
  36.2 48.6 %copy-start.105 = (pred[515]{0:T(1024)(128)(4,1)}, pred[515]{0:T(1024)(128)(4,1)S(1)}, u32[]{:S(2)}) copy-start(pred[515]{0:T(1024)(128)(4,1)S(1)} %get-tuple-element.2403) | copy-start | bytes 1549
  36.2 48.6 %copy-start.107 = (pred[515]{0:T(1024)(128)(4,1)}, pred[515]{0:T(1024)(128)(4,1)S(1)}, u32[]{:S(2)}) copy-start(pred[515]{0:T(1024)(128)(4,1)S(1)} %get-tuple-element.2404) | copy-start | bytes 1549
  36.2 48.6 %copy-start.109 = (pred[515]{0:T(1024)(128)(4,1)}, pred[515]{0:T(1024)(128)(4,1)S(1)}, u32[]{:S(2)}) copy-start(pred[515]{0:T(1024)(128)(4,1)S(1)} %get-tuple-element.2405) | copy-start | bytes 1549
  37.2 47.6 %copy-start.80 = (f32[1664]{0:T(1024)}, f32[1664]{0:T(1024)S(1)}, u32[]{:S(2)}) copy-start(f32[1664]{0:T(1024)S(1)} %get-tuple-element.2197) | copy-start | bytes 19972
  37.2 47.6 %copy-start.82 = (f32[1664]{0:T(1024)}, f32[1664]{0:T(1024)S(1)}, u32[]{:S(2)}) copy-start(f32[1664]{0:T(1024)S(1)} %get-tuple-element.2198) | copy-start | bytes 19972
  37.2 47.6 %copy-start.84 = (f32[1664]{0:T(1024)}, f32[1664]{0:T(1024)S(1)}, u32[]{:S(2)}) copy-start(f32[1664]{0:T(1024)S(1)} %get-tuple-element.2199) | copy-start | bytes 19972
  37.2 47.6 %copy-start.86 = (f32[1664]{0:T(1024)}, f32[1664]{0:T(1024)S(1)}, u32[]{:S(2)}) copy-start(f32[1664]{0:T(1024)S(1)} %get-tuple-element.2200) | copy-start | bytes 19972
  56.2 15.8 %copy-start.49 = (bf16[768,48]{1,0:T(8,128)(2,1)}, bf16[768,48]{1,0:T(8,128)(2,1)S(1)}, u32[]{:S(2)}) copy-start(bf16[768,48]{1,0:T(8,128)(2,1)S(1)} %all_gather.12) | copy-start | bytes 221188
  57.8 25.9 %copy-start.42 = (bf16[512,128]{1,0:T(8,128)(2,1)}, bf16[512,128]{1,0:T(8,128)(2,1)S(1)}, u32[]{:S(2)}) copy-start(bf16[512,128]{1,0:T(8,128)(2,1)S(1)} %convolution_convert_fusion.1) | copy-start | bytes 393220
  59.0 13.1 copy-start.118
  59.8 19.6 %copy-start.56 = (f32[512,24]{0,1:T(8,128)}, f32[512,24]{0,1:T(8,128)S(1)}, u32[]{:S(2)}) copy-start(f32[512,24]{0,1:T(8,128)S(1)} %get-tuple-element.2354) | copy-start | bytes 147460
  59.8 20.1 %copy-start.52 = (f32[512,24]{0,1:T(8,128)}, f32[512,24]{0,1:T(8,128)S(1)}, u32[]{:S(2)}) copy-start(f32[512,24]{0,1:T(8,128)S(1)} %get-tuple-element.2398) | copy-start | bytes 147460
  75.0 8.7 collective-permute-start
  81.6 245.5 %copy-start.78 = (f32[1536]{0:T(1024)}, f32[1536]{0:T(1024)S(1)}, u32[]{:S(2)}) copy-start(f32[1536]{0:T(1024)S(1)} %mul.1288) | copy-start | bytes 18436
  91.6 32.3 %copy-start.37 = (f32[512,64]{1,0:T(8,128)}, f32[512,64]{1,0:T(8,128)S(1)}, u32[]{:S(2)}) copy-start(f32[512,64]{1,0:T(8,128)S(1)} %get-tuple-element.2390) | copy-start | bytes 393220
  91.6 32.5 %copy-start.36 = (f32[512,64]{1,0:T(8,128)}, f32[512,64]{1,0:T(8,128)S(1)}, u32[]{:S(2)}) copy-start(f32[512,64]{1,0:T(8,128)S(1)} %get-tuple-element.2389) | copy-start | bytes 393220
  199.2 9.2 copy-start.28
  199.2 9.1 copy-start.33
  199.2 9.1 copy-start.34
  213.0 64.1 %copy-start.54 = (f32[512,24]{0,1:T(8,128)S(1)}, f32[512,24]{0,1:T(8,128)}, u32[]{:S(2)}) copy-start(f32[512,24]{0,1:T(8,128)} %rev.112) | copy-start | bytes 147460
  277.1 41.3 %collective-permute-start.1 = (bf16[1,24,64,64]{3,2,1,0:T(8,128)(2,1)}, bf16[1,24,64,64]{3,2,1,0:T(8,128)(2,1)}, u32[]{:S(2)}, u32[]{:S(2)}) collective-permute-start(bf16[1,24,64,64]{3,2,1,0:T(8,128)(2,1)} %fusion.246), channel_id=1, source_target_pairs={{0,16},{16,0},{1,17},{17,1},{2,18},{18,2},{3,19},{19,3},{4,20},{20... | collective-permute-start | bytes 589832 | tf_op jit(solution)/shard_map/ppermute | solution.py:26
  327.1 8.8 copy-start.30
  327.1 8.8 copy-start.76
  334.3 10.4 copy-start.94
  350.9 29.1 %copy-start.1 = (bf16[512,1536]{1,0:T(8,128)(2,1)}, bf16[512,1536]{1,0:T(8,128)(2,1)S(1)}, u32[]{:S(2)}) copy-start(bf16[512,1536]{1,0:T(8,128)(2,1)S(1)} %get-tuple-element.2344) | copy-start | bytes 4718596
  366.0 52.9 %collective-permute-start.2 = (bf16[1,24,64,64]{3,2,1,0:T(8,128)(2,1)}, bf16[1,24,64,64]{3,2,1,0:T(8,128)(2,1)}, u32[]{:S(2)}, u32[]{:S(2)}) collective-permute-start(bf16[1,24,64,64]{3,2,1,0:T(8,128)(2,1)} %fusion.230), channel_id=1, source_target_pairs={{0,16},{16,0},{1,17},{17,1},{2,18},{18,2},{3,19},{19,3},{4,20},{20... | collective-permute-start | bytes 589832 | tf_op jit(solution)/shard_map/ppermute | solution.py:26
  395.9 13.4 copy-start.17
  747.0 24.7 %copy-start.45 = (f32[4,128,64]{2,1,0:T(8,128)S(1)}, f32[4,128,64]{2,1,0:T(8,128)}, u32[]{:S(2)}) copy-start(f32[4,128,64]{2,1,0:T(8,128)} %copy.522) | copy-start | bytes 393220
  747.0 24.7 %copy-start.46 = (f32[512,64]{1,0:T(8,128)S(1)}, f32[512,64]{1,0:T(8,128)}, u32[]{:S(2)}) copy-start(f32[512,64]{1,0:T(8,128)} %rev.114) | copy-start | bytes 393220
  747.0 24.7 %copy-start.2 = (bf16[512,1536]{1,0:T(8,128)(2,1)S(1)}, bf16[512,1536]{1,0:T(8,128)(2,1)}, u32[]{:S(2)}) copy-start(bf16[512,1536]{1,0:T(8,128)(2,1)} %copy-done.1) | copy-start | bytes 4718596
  747.0 24.7 %copy-start.79 = (f32[1536]{0:T(1024)S(1)}, f32[1536]{0:T(1024)}, u32[]{:S(2)}) copy-start(f32[1536]{0:T(1024)} %copy-done.78) | copy-start | bytes 18436
  790.2 5.7 collective-permute-start.3
  804.5 605.3 %all-reduce.34.cloned.1.call-start = ((), (), s32[]{:S(2)}) async-start(), calls=%async_computation.3 | async-start | bytes 29392896 | tf_op jit(solution)/shard_map/psum | solution.py:267
  1079.0 76.9 %copy-start.98 = (f32[512]{0:T(512)S(1)}, f32[512]{0:T(512)}, u32[]{:S(2)}) copy-start(f32[512]{0:T(512)} %copy-done.97) | copy-start | bytes 6148
  1079.0 76.9 %copy-start.32 = (bf16[1,512,768]{2,1,0:T(8,128)(2,1)S(1)}, bf16[1,512,768]{2,1,0:T(8,128)(2,1)}, u32[]{:S(2)}) copy-start(bf16[1,512,768]{2,1,0:T(8,128)(2,1)} %param.38) | copy-start | bytes 2359300
  1409.7 10.2 slice-start
  1409.7 9.5 copy-start.69
  1409.7 10.2 slice-start.1
  (135 other events, 627.0 us)
Sparse Core Ops, SparseCore 0:
  10.3 57.0 all-gather.2
  69.7 41.3 all-gather.4
  804.6 265.9 all-reduce.31
  1073.2 336.4 all-reduce.33
